TPU v7x, 32 devices: a whole 2x2x4 slice. The times are simulated.
32 devices in a mesh: tile: 4 (over y, x), slab: 8 (over z, core).
Axes of the slice: x: 2, y: 2, z: 4, core: 2. Of those that a mesh axis runs over, the one named last changes fastest.
Arguments:
- raw_stack: bfloat16 [32, 120, 2048], P('slab', None, 'tile'), may hold values from -48 to 48
- shear_offsets: int32 [32], P('slab'), may hold values from 0 to 8
- intersection_widths: int32 [3], replicated, may hold values from 32 to 128
Outputs:
- difference: bfloat16 [128, 32, 2048], P('slab', None, 'tile')
- level_one: bfloat16 [64, 16, 1024], P('slab', None, 'tile')
- level_two: bfloat16 [32, 8, 512], P('slab', None, 'tile')
All inputs are finite; a program needn't handle non-finite values.
Results may differ from a plain program's by a relative error of at most 0.003.
Values may be sent and summed in bfloat16 or wider, within the bound.
No kernel may reach another device: no remote copies, remote signals or barrier semaphores. Data moves between devices by JAX's collectives and lax.ppermute only.
A program may use at most 64 MiB of HBM per device.

v0:
```python
import math
import jax
import jax.numpy as jnp
from jax import lax
from jax.sharding import PartitionSpec as P

SLAB_ROWS = 16
STRIP = 6
RADIUS = 4


def padded_2(block, sides, width):
    for axis, dim in sides:
        count = lax.axis_size(axis)
        forward = [(i, i + 1) for i in range(count - 1)]
        backward = [(target, source) for source, target in forward]
        low = lax.ppermute(
            lax.slice_in_dim(block, block.shape[dim] - width, None, axis=dim), axis, forward
        )
        high = lax.ppermute(lax.slice_in_dim(block, 0, width, axis=dim), axis, backward)
        block = jnp.concatenate([low, block, high], axis=dim)
    return block


def shifted(block, axis, distance):
    devices = range(lax.axis_size(axis))
    route = [(i - distance, i) for i in devices if i - distance in devices]
    return lax.ppermute(block, axis, route)


def gauss_taps(sigma_value, reach_cells):
    entries = [
        math.exp(-(offset * offset) / (2.0 * sigma_value * sigma_value))
        for offset in range(-reach_cells, reach_cells + 1)
    ]
    weight_sum = sum(entries)
    return [entry_value / weight_sum for entry_value in entries]


def binomial_taps():
    return [1.0 / 16.0, 4.0 / 16.0, 6.0 / 16.0, 4.0 / 16.0, 1.0 / 16.0]


def smooth(source, weights, direction, begin_at, length_out, stride):
    result = weights[0] * lax.slice_in_dim(
        source, begin_at, begin_at + (length_out - 1) * stride + 1, stride, direction
    )
    for offset in range(1, len(weights)):
        lowest = begin_at + offset
        window = lax.slice_in_dim(
            source, lowest, lowest + (length_out - 1) * stride + 1, stride, direction
        )
        result = result + weights[offset] * window
    return result


def pad_scans(source, width_cells):
    return jnp.pad(source, ((0, 0), (width_cells, width_cells), (0, 0)))


def deskew(planes_block, shifts, shear_top, total_rows, margin):
    padded = jnp.pad(planes_block, ((0, 0), (shear_top + margin, shear_top + margin), (0, 0)))

    def place_plane(plane, shift_value):
        return lax.dynamic_slice_in_dim(plane, shear_top - shift_value, total_rows + 2 * margin, 0)

    return jax.vmap(place_plane, out_axes=1)(padded, shifts)


def band_table(weights, source_pos, target_pos):
    reach_cells = len(weights) // 2
    offsets = source_pos[:, None] - target_pos[None, :] + reach_cells
    table = jnp.zeros(offsets.shape, jnp.float32)
    for index_tap in range(len(weights)):
        table = table + weights[index_tap] * (offsets == index_tap).astype(jnp.float32)
    return table


def along_columns(pieces, tables):
    total = None
    for piece_field, table in zip(pieces, tables):
        term = jnp.einsum("rsc,co->rso", piece_field, table, precision=lax.Precision.HIGHEST)
        total = term if total is None else total + term
    return total


def body(raw_stack, shear_offsets, intersection_widths):
    slab_count = lax.axis_size("slab")
    tile_count = lax.axis_size("tile")
    tile_index = lax.axis_index("tile")
    planes, camera, columns = raw_stack.shape
    total_rows = SLAB_ROWS * slab_count
    shear_top = total_rows - camera
    row_depth = RADIUS
    deskewed = deskew(raw_stack, shear_offsets, shear_top, total_rows, 0)
    outgoing = deskewed.reshape(slab_count, SLAB_ROWS, planes, columns)
    volume = lax.all_to_all(outgoing, "slab", split_axis=0, concat_axis=2, tiled=True)[0]
    volume = padded_2(volume, (("slab", 0),), row_depth)
    right_width = intersection_widths[jnp.minimum(tile_index, tile_count - 2)]
    left_width = intersection_widths[jnp.maximum(tile_index - 1, 0)]
    toward_right = lax.dynamic_slice_in_dim(volume, columns - right_width - STRIP, STRIP, 2)
    toward_left = lax.dynamic_slice_in_dim(volume, left_width, STRIP, 2)
    from_left = shifted(toward_right, "tile", 1)
    from_right = shifted(toward_left, "tile", -1)
    pieces = (
        volume.astype(jnp.float32),
        from_left.astype(jnp.float32),
        from_right.astype(jnp.float32),
    )
    own_pos = jnp.arange(columns, dtype=jnp.int32)
    left_pos = jnp.arange(STRIP, dtype=jnp.int32) - STRIP
    right_pos = jnp.arange(STRIP, dtype=jnp.int32) + columns
    sources = (own_pos, left_pos, right_pos)
    scan_count = volume.shape[1]

    def gaussian(sigma_value):
        weights = gauss_taps(sigma_value, RADIUS)
        colled = along_columns(pieces, [band_table(weights, place, own_pos) for place in sources])
        along_rows = smooth(colled, weights, 0, row_depth - RADIUS, SLAB_ROWS, 1)
        return smooth(pad_scans(along_rows, RADIUS), weights, 1, 0, scan_count, 1)

    difference = (gaussian(1.0) - gaussian(1.6)).astype(jnp.bfloat16)
    binomial = binomial_taps()
    main_pos = 2 * jnp.arange(columns // 2, dtype=jnp.int32)
    edge_pos = jnp.array([-4, -2, columns, columns + 2], dtype=jnp.int32)
    target_pos = jnp.concatenate([main_pos, edge_pos])
    colled = along_columns(pieces, [band_table(binomial, place, target_pos) for place in sources])
    row_keep = jnp.ones((SLAB_ROWS // 2,), dtype=bool)
    coarse_count = SLAB_ROWS // 2
    rows_blur = smooth(colled, binomial, 0, row_depth - 2, coarse_count, 2)
    scans_blur = smooth(pad_scans(rows_blur, 2), binomial, 1, 0, scan_count // 2, 2)
    edge_keep = ((edge_pos >= 0) | (tile_index > 0)) & (
        (edge_pos < columns) | (tile_index < tile_count - 1)
    )
    main_ext = jnp.where(row_keep[:, None, None], scans_blur[:, :, 0 : columns // 2], 0.0).astype(
        jnp.bfloat16
    )
    edge_mask = row_keep[:, None, None] & edge_keep[None, None, :]
    edge_ext = jnp.where(edge_mask, scans_blur[:, :, columns // 2 :], 0.0).astype(jnp.bfloat16)
    main_index = jnp.arange(columns // 2, dtype=jnp.int32) + 2
    edge_index = jnp.array([0, 1, columns // 2 + 2, columns // 2 + 3], dtype=jnp.int32)
    coarse_target = 2 * jnp.arange(columns // 4, dtype=jnp.int32) + 2
    coarse_cols = along_columns(
        (main_ext.astype(jnp.float32), edge_ext.astype(jnp.float32)),
        [
            band_table(binomial, main_index, coarse_target),
            band_table(binomial, edge_index, coarse_target),
        ],
    )
    coarse_cols = padded_2(coarse_cols, (("slab", 0),), 2)
    rows_two = smooth(coarse_cols, binomial, 0, 0, SLAB_ROWS // 4, 2)
    level_two = smooth(pad_scans(rows_two, 2), binomial, 1, 0, scan_count // 4, 2).astype(
        jnp.bfloat16
    )
    return (difference, main_ext, level_two)


def solution(mesh):
    placed = (P("slab", None, "tile"), P("slab"), P())
    return jax.shard_map(
        body,
        mesh=mesh,
        in_specs=placed,
        out_specs=(P("slab", None, "tile"), P("slab", None, "tile"), P("slab", None, "tile")),
        check_vma=False,
    )
```

profile of v0, /device:TPU:1, one launch (start us, length us, event | category | flops | bytes accessed | tf_op | source)
XLA Modules:
  0.0 147.0 jit_solution(10012603302796135666)
XLA Ops:
  2.8 3.7 %gather_fusion = bf16[4,128,512]{2,0,1:T(4,128)(2,1)} fusion(bf16[4,136,512]{2,0,1:T(4,128)(2,1)S(1)} %pad.20, s32[4]{0:T(128)S(1)} %fusion.504), kind=kCustom, calls=%fused_computation | custom fusion | bytes 1048624 | tf_op jit(solution)/shard_map/vmap()/gather | solution.py:65
  6.5 6.5 %all-to-all-start = ((bf16[8,16,4,512]{3,2,1,0:T(4,128)(2,1)}), bf16[8,16,4,512]{3,2,1,0:T(4,128)(2,1)S(1)}, u32[]{:S(2)}, u32[]{:S(2)}) async-start(bf16[8,16,4,512]{3,2,1,0:T(4,128)(2,1)} %bitcast.3), calls=%async_computation | async-start | bytes 1048576 | tf_op jit(solution)/shard_map/all_to_all | solution.py:97
  13.1 14.4 %all-to-all-done = bf16[8,16,4,512]{3,2,1,0:T(4,128)(2,1)S(1)} async-done(((bf16[8,16,4,512]{3,2,1,0:T(4,128)(2,1)}), bf16[8,16,4,512]{3,2,1,0:T(4,128)(2,1)S(1)}, u32[]{:S(2)}, u32[]{:S(2)}) %all-to-all-start) | async-done | bytes 524320 | tf_op jit(solution)/shard_map/all_to_all | solution.py:97
  36.5 3.8 %collective-permute-done.1 = bf16[4,32,512]{2,1,0:T(8,128)(2,1)S(1)} collective-permute-done((bf16[4,32,512]{2,1,0:T(8,128)(2,1)S(1)}, bf16[4,32,512]{2,1,0:T(8,128)(2,1)S(1)}, u32[]{:S(2)}, u32[]{:S(2)}) %collective-permute-start.1) | collective-permute-done | bytes 131104 | tf_op jit(solution)/shard_map/ppermute | solution.py:20
  40.3 2.7 %fusion.50 = f32[24,32,512]{2,1,0:T(8,128)} fusion(bf16[24,32,512]{2,1,0:T(8,128)(2,1)S(1)} %constant_dynamic-update-slice_fusion), kind=kOutput, calls=%fused_computation.92 | convolution fusion | flops 2423259136 | bytes 2359296 | tf_op jit(solution)/shard_map/rsc,co->rso/dot_general | solution.py:82
  43.0 2.7 %fusion.52 = f32[24,32,512]{2,1,0:T(8,128)} fusion(bf16[24,32,512]{2,1,0:T(8,128)(2,1)S(1)} %constant_dynamic-update-slice_fusion), kind=kOutput, calls=%fused_computation.94 | convolution fusion | flops 2423259136 | bytes 2359296 | tf_op jit(solution)/shard_map/rsc,co->rso/dot_general | solution.py:82
  45.9 3.1 %collective-permute-start.2 = (bf16[24,32,6]{2,1,0:T(8,128)(2,1)S(1)}, bf16[24,32,6]{2,1,0:T(8,128)(2,1)S(1)}, u32[]{:S(2)}, u32[]{:S(2)}) collective-permute-start(bf16[24,32,6]{2,1,0:T(8,128)(2,1)S(1)} %get-tuple-element.7), channel_id=1, source_target_pairs={{0,8},{8,16},{16,24},{1,9},{9,17},{17,25},{2,10},{10,18},{18,26},{... | collective-permute-start | bytes 27656 | tf_op jit(solution)/shard_map/ppermute | solution.py:28
  52.3 3.8 %copy.37 = f32[24,32,260]{1,0,2:T(8,128)} copy(f32[24,32,260]{2,1,0:T(8,128)S(1)} %fusion.115) | data formatting | bytes 1597440 | tf_op jit(solution)/shard_map/rsc,co->rso/dot_general | solution.py:82
  58.2 3.7 %copy.40 = f32[24,32,260]{1,0,2:T(8,128)} copy(f32[24,32,260]{2,1,0:T(8,128)S(1)} %fusion.343) | data formatting | bytes 1597440 | tf_op jit(solution)/shard_map/rsc,co->rso/dot_general | solution.py:82
  62.6 3.8 %copy.38 = f32[24,32,260]{1,0,2:T(8,128)} copy(f32[24,32,260]{2,1,0:T(8,128)S(1)} %fusion.345) | data formatting | bytes 1597440 | tf_op jit(solution)/shard_map/rsc,co->rso/dot_general | solution.py:82
  66.4 4.2 %add_add_fusion = f32[24,32,260]{1,0,2:T(8,128)S(1)} fusion(f32[24,32,260]{1,0,2:T(8,128)} %copy.40, f32[24,32,260]{1,0,2:T(8,128)} %copy.37, f32[24,32,260]{1,0,2:T(8,128)} %copy.38), kind=kLoop, calls=%fused_computation.1 | loop fusion | flops 399360 | bytes 3194880 | tf_op jit(solution)/shard_map/add | solution.py:83
  70.6 4.1 %slice.231 = f32[8,32,260]{1,0,2:T(8,128)} slice(f32[24,32,260]{1,0,2:T(8,128)S(1)} %add_add_fusion), slice={[6:21:2], [0:32:1], [0:260:1]} | slice | bytes 532480 | tf_op jit(solution)/shard_map/slice | solution.py:50
  74.7 4.1 %slice.230 = f32[8,32,260]{1,0,2:T(8,128)} slice(f32[24,32,260]{1,0,2:T(8,128)S(1)} %add_add_fusion), slice={[5:20:2], [0:32:1], [0:260:1]} | slice | bytes 532480 | tf_op jit(solution)/shard_map/slice | solution.py:50
  78.7 4.0 %slice.229 = f32[8,32,260]{1,0,2:T(8,128)} slice(f32[24,32,260]{1,0,2:T(8,128)S(1)} %add_add_fusion), slice={[4:19:2], [0:32:1], [0:260:1]} | slice | bytes 532480 | tf_op jit(solution)/shard_map/slice | solution.py:50
  82.8 4.0 %slice.228 = f32[8,32,260]{1,0,2:T(8,128)} slice(f32[24,32,260]{1,0,2:T(8,128)S(1)} %add_add_fusion), slice={[3:18:2], [0:32:1], [0:260:1]} | slice | bytes 532480 | tf_op jit(solution)/shard_map/slice | solution.py:50
  86.8 4.1 %slice.227 = f32[8,32,260]{1,0,2:T(8,128)} slice(f32[24,32,260]{1,0,2:T(8,128)S(1)} %add_add_fusion), slice={[2:17:2], [0:32:1], [0:260:1]} | slice | bytes 532480 | tf_op jit(solution)/shard_map/slice | solution.py:45
  90.9 2.8 %multiply_add_fusion.1 = f32[8,32,260]{1,0,2:T(8,128)S(1)} fusion(f32[8,32,260]{1,0,2:T(8,128)} %slice.231, f32[8,32,260]{1,0,2:T(8,128)} %slice.230, f32[8,32,260]{1,0,2:T(8,128)} %slice.229, f32[8,32,260]{1,0,2:T(8,128)} %slice.228, f32[8,32,260]{1,0,2:T(8,128)} %slice.227), kind=kLoop, calls=%fused_computation.22 | loop fusion | flops 599040 | bytes 1597440 | tf_op jit(solution)/shard_map/add | solution.py:53
  94.0 6.1 %slice.236 = f32[8,16,260]{1,0,2:T(8,128)S(1)} slice(f32[8,36,260]{1,0,2:T(8,128)S(1)} %pad.23), slice={[0:8:1], [4:35:2], [0:260:1]} | slice | bytes 266240 | tf_op jit(solution)/shard_map/slice | solution.py:50
  100.1 6.1 %slice.235 = f32[8,16,260]{1,0,2:T(8,128)S(1)} slice(f32[8,36,260]{1,0,2:T(8,128)S(1)} %pad.23), slice={[0:8:1], [3:34:2], [0:260:1]} | slice | bytes 266240 | tf_op jit(solution)/shard_map/slice | solution.py:50
  106.2 6.6 %slice.234 = f32[8,16,260]{1,0,2:T(8,128)} slice(f32[8,36,260]{1,0,2:T(8,128)S(1)} %pad.23), slice={[0:8:1], [2:33:2], [0:260:1]} | slice | bytes 266240 | tf_op jit(solution)/shard_map/slice | solution.py:50
  112.7 6.6 %slice.233 = f32[8,16,260]{1,0,2:T(8,128)} slice(f32[8,36,260]{1,0,2:T(8,128)S(1)} %pad.23), slice={[0:8:1], [1:32:2], [0:260:1]} | slice | bytes 266240 | tf_op jit(solution)/shard_map/slice | solution.py:50
  119.3 6.4 %slice.232 = f32[8,16,260]{1,0,2:T(8,128)} slice(f32[8,36,260]{1,0,2:T(8,128)S(1)} %pad.23), slice={[0:8:1], [0:31:2], [0:260:1]} | slice | bytes 266240 | tf_op jit(solution)/shard_map/slice | solution.py:45
  130.9 5.2 %collective-permute-start.4 = (f32[2,16,128]{2,1,0:T(8,128)S(1)}, f32[2,16,128]{2,1,0:T(8,128)S(1)}, u32[]{:S(2)}, u32[]{:S(2)}) collective-permute-start(f32[2,16,128]{2,1,0:T(8,128)S(1)} %get-tuple-element.10), channel_id=1, source_target_pairs={{0,1},{1,2},{2,3},{3,4},{4,5},{5,6},{6,7},{8,9},{9,10},{10,11},{11... | collective-permute-start | bytes 49160 | tf_op jit(solution)/shard_map/ppermute | solution.py:17
  143.3 3.0 %fusion.10 = bf16[16,32,512]{2,1,0:T(8,128)(2,1)} fusion(f32[16,32,512]{2,1,0:T(8,128)S(1)} %get-tuple-element.15, f32[16,32,512]{2,1,0:T(8,128)S(1)} %get-tuple-element.14), kind=kLoop, calls=%fused_computation.33 | loop fusion | flops 9437184 | bytes 2621440 | tf_op jit(solution)/shard_map/convert_element_type | solution.py:122
  (76 shorter events, 27.4 us)
Async XLA Ops:
  6.5 6.6 %copy-start.8 = (pred[4]{0:T(512)(128)(4,1)S(1)}, pred[4]{0:T(512)(128)(4,1)}, u32[]{:S(2)}) copy-start(pred[4]{0:T(512)(128)(4,1)} %constant.255) | copy-start | bytes 16
  6.5 6.6 %copy-start.9 = (pred[4]{0:T(512)(128)(4,1)S(1)}, pred[4]{0:T(512)(128)(4,1)}, u32[]{:S(2)}) copy-start(pred[4]{0:T(512)(128)(4,1)} %constant.254) | copy-start | bytes 16
  6.5 23.2 %copy-start.5 = (s32[3]{0:T(128)S(1)}, s32[3]{0:T(128)}, u32[]{:S(2)}) copy-start(s32[3]{0:T(128)} %param.7) | copy-start | bytes 40
  6.5 27.0 %copy-start.7 = (s32[4]{0:T(128)S(1)}, s32[4]{0:T(128)}, u32[]{:S(2)}) copy-start(s32[4]{0:T(128)} %constant.238.clone) | copy-start | bytes 52
  6.5 21.0 %all-to-all-start = ((bf16[8,16,4,512]{3,2,1,0:T(4,128)(2,1)}), bf16[8,16,4,512]{3,2,1,0:T(4,128)(2,1)S(1)}, u32[]{:S(2)}, u32[]{:S(2)}) async-start(bf16[8,16,4,512]{3,2,1,0:T(4,128)(2,1)} %bitcast.3), calls=%async_computation | async-start | bytes 1048576 | tf_op jit(solution)/shard_map/all_to_all | solution.py:97
  27.7 8.7 %collective-permute-start = (bf16[4,32,512]{2,1,0:T(8,128)(2,1)S(1)}, bf16[4,32,512]{2,1,0:T(8,128)(2,1)S(1)}, u32[]{:S(2)}, u32[]{:S(2)}) collective-permute-start(bf16[4,32,512]{2,1,0:T(8,128)(2,1)S(1)} %slice.190), channel_id=1, source_target_pairs={{0,1},{1,2},{2,3},{3,4},{4,5},{5,6},{6,7},{8,9},{9,10},{10,11},{11... | collective-permute-start | bytes 393224 | tf_op jit(solution)/shard_map/ppermute | solution.py:17
  34.0 6.3 %collective-permute-start.1 = (bf16[4,32,512]{2,1,0:T(8,128)(2,1)S(1)}, bf16[4,32,512]{2,1,0:T(8,128)(2,1)S(1)}, u32[]{:S(2)}, u32[]{:S(2)}) collective-permute-start(bf16[4,32,512]{2,1,0:T(8,128)(2,1)S(1)} %slice.192), channel_id=1, source_target_pairs={{1,0},{2,1},{3,2},{4,3},{5,4},{6,5},{7,6},{9,8},{10,9},{11,10},{12... | collective-permute-start | bytes 393224 | tf_op jit(solution)/shard_map/ppermute | solution.py:20
  45.9 16.0 %collective-permute-start.2 = (bf16[24,32,6]{2,1,0:T(8,128)(2,1)S(1)}, bf16[24,32,6]{2,1,0:T(8,128)(2,1)S(1)}, u32[]{:S(2)}, u32[]{:S(2)}) collective-permute-start(bf16[24,32,6]{2,1,0:T(8,128)(2,1)S(1)} %get-tuple-element.7), channel_id=1, source_target_pairs={{0,8},{8,16},{16,24},{1,9},{9,17},{17,25},{2,10},{10,18},{18,26},{... | collective-permute-start | bytes 27656 | tf_op jit(solution)/shard_map/ppermute | solution.py:28
  49.0 8.5 %collective-permute-start.3 = (bf16[24,32,6]{2,1,0:T(8,128)(2,1)S(1)}, bf16[24,32,6]{2,1,0:T(8,128)(2,1)S(1)}, u32[]{:S(2)}, u32[]{:S(2)}) collective-permute-start(bf16[24,32,6]{2,1,0:T(8,128)(2,1)S(1)} %get-tuple-element.6), channel_id=1, source_target_pairs={{8,0},{16,8},{24,16},{9,1},{17,9},{25,17},{10,2},{18,10},{26,18},{... | collective-permute-start | bytes 27656 | tf_op jit(solution)/shard_map/ppermute | solution.py:28
  61.9 0.7 copy-start
  127.9 0.8 copy-start.6
  127.9 8.2 %copy-start.1 = (bf16[24,32,6]{2,1,0:T(8,128)(2,1)S(1)}, bf16[24,32,6]{2,1,0:T(8,128)(2,1)}, u32[]{:S(2)}) copy-start(bf16[24,32,6]{2,1,0:T(8,128)(2,1)} %copy-done) | copy-start | bytes 27652
  128.3 8.7 %copy-start.4 = (bf16[8,16,256]{2,1,0:T(8,128)(2,1)}, bf16[8,16,256]{2,1,0:T(8,128)(2,1)S(1)}, u32[]{:S(2)}) copy-start(bf16[8,16,256]{2,1,0:T(8,128)(2,1)S(1)} %copy.43) | copy-start | bytes 196612
  129.0 17.3 %collective-permute-start.5 = (f32[2,16,128]{2,1,0:T(8,128)S(1)}, f32[2,16,128]{2,1,0:T(8,128)S(1)}, u32[]{:S(2)}, u32[]{:S(2)}) collective-permute-start(f32[2,16,128]{2,1,0:T(8,128)S(1)} %get-tuple-element.11), channel_id=1, source_target_pairs={{1,0},{2,1},{3,2},{4,3},{5,4},{6,5},{7,6},{9,8},{10,9},{11,10},{12... | collective-permute-start | bytes 49160 | tf_op jit(solution)/shard_map/ppermute | solution.py:20
  130.9 15.4 %collective-permute-start.4 = (f32[2,16,128]{2,1,0:T(8,128)S(1)}, f32[2,16,128]{2,1,0:T(8,128)S(1)}, u32[]{:S(2)}, u32[]{:S(2)}) collective-permute-start(f32[2,16,128]{2,1,0:T(8,128)S(1)} %get-tuple-element.10), channel_id=1, source_target_pairs={{0,1},{1,2},{2,3},{3,4},{4,5},{5,6},{6,7},{8,9},{9,10},{10,11},{11... | collective-permute-start | bytes 49160 | tf_op jit(solution)/shard_map/ppermute | solution.py:17
  137.0 1.4 copy-start.3
  138.4 1.4 copy-start.2
where the time goes:
time: 148 us; the launch traced here: 147 us
  local copies, waits for them, and re-layouts  71.6 us (48%)
  starting transfers between devices  22.6 us (15%)
  waiting for transfers between devices  19.7 us (13%)
  other arithmetic  16.2 us (11%)
  matrix products  12.6 us (9%)
  between operations  4.31 us (3%)
    slice x12, local copies, waits for them, and re-layouts, smooth(): lax.slice_in_dim(source, lowest, lowest + (length_out - 1) * stride + 1,...  41.5 us
    all_to_all x1, waiting for transfers between devices, body(): lax.all_to_all(outgoing, 'slab', split_axis=0, concat_axis=2, tiled=True)[0]  14.4 us
    dot_general x11, matrix products, along_columns(): jnp.einsum('rsc,co->rso', piece_field, table, precision=lax.Precision.HIG...  12.6 us
    dot_general x3, local copies, waits for them, and re-layouts, along_columns(): jnp.einsum('rsc,co->rso', piece_field, table, precision=lax.Precision.HIG...  11.3 us
    slice x3, local copies, waits for them, and re-layouts, smooth(): lax.slice_in_dim(source, begin_at, begin_at + (length_out - 1) * stride +...  10.4 us
    add x4, other arithmetic, smooth(): result = result + weights[offset] * window  7.57 us
    ppermute x2, starting transfers between devices, padded_2(): lax.ppermute(lax.slice_in_dim(block, block.shape[dim] - width, None, axis...  7.1 us
    all_to_all x1, starting transfers between devices, body(): lax.all_to_all(outgoing, 'slab', split_axis=0, concat_axis=2, tiled=True)[0]  6.52 us
  transfers between devices with their start and end apart: 7, of which 3 were waited for; matrix products, arithmetic and copies ran while one was open for 14% of the time, Pallas kernels for 0%

commit v1 on v0

--- a/solution.py
+++ b/solution.py
@@ -7,6 +7,22 @@
 SLAB_ROWS = 16
 STRIP = 6
 RADIUS = 4
+
+
+def swapped_with_each(array, axis, split, join):
+    ways, here = (lax.axis_size(axis), lax.axis_index(axis))
+    width = array.shape[split] // ways
+    shape = list(array.shape)
+    shape[split] = width
+    height = shape[join]
+    shape[join] = height * ways
+    full = jnp.zeros(shape, array.dtype)
+    for mask in range(ways):
+        part = lax.dynamic_slice_in_dim(array, (here ^ mask) * width, width, axis=split)
+        if mask:
+            part = lax.ppermute(part, axis, [(d, d ^ mask) for d in range(ways)])
+        full = lax.dynamic_update_slice_in_dim(full, part, (here ^ mask) * height, axis=join)
+    return full
 
 
 def padded_2(block, sides, width):
@@ -94,7 +110,7 @@
     row_depth = RADIUS
     deskewed = deskew(raw_stack, shear_offsets, shear_top, total_rows, 0)
     outgoing = deskewed.reshape(slab_count, SLAB_ROWS, planes, columns)
-    volume = lax.all_to_all(outgoing, "slab", split_axis=0, concat_axis=2, tiled=True)[0]
+    volume = swapped_with_each(outgoing, "slab", 0, 2)[0]
     volume = padded_2(volume, (("slab", 0),), row_depth)
     right_width = intersection_widths[jnp.minimum(tile_index, tile_count - 2)]
     left_width = intersection_widths[jnp.maximum(tile_index - 1, 0)]

time: 148 us -> 139 us (0.939)
  waiting for transfers between devices: 19.7 us -> 6.02 us
  starting transfers between devices: 22.6 us -> 26.7 us
    all_to_all x1 -> x0, waiting for transfers between devices: 14.4 us -> none  [body(): lax.all_to_all(outgoing, 'slab', split_axis=0, concat_axis=2, tiled=True)[0]]
    ppermute x0 -> x7, starting transfers between devices: none -> 9.67 us  [swapped_with_each(): part = lax.ppermute(part, axis, [(d, d ^ mask) for d in range(ways)])]
    all_to_all x1 -> x0, starting transfers between devices: 6.52 us -> none  [body(): lax.all_to_all(outgoing, 'slab', split_axis=0, concat_axis=2, tiled=True)[0]]
    ppermute x0 -> x7, waiting for transfers between devices: none -> 6 us  [swapped_with_each(): part = lax.ppermute(part, axis, [(d, d ^ mask) for d in range(ways)])]
    ppermute x2, waiting for transfers between devices: 3.79 us -> 0.01 us  [padded_2(): lax.ppermute(lax.slice_in_dim(block, 0, width, axis=dim), axis, backward)]
  transfers between devices with their start and end apart: 7 -> 13, of which waited for: 3 -> 1; matrix products, arithmetic and copies ran while one was open for 14% -> 19% of each run, Pallas kernels for 0% -> 0%
where the time goes in v1:
time: 139 us; the launch traced here: 137 us
  local copies, waits for them, and re-layouts  71 us (51%)
  starting transfers between devices  26.7 us (19%)
  other arithmetic  16.5 us (12%)
  matrix products  12.7 us (9%)
  waiting for transfers between devices  6.02 us (4%)
  between operations  4.48 us (3%)
    slice x12, local copies, waits for them, and re-layouts, smooth(): lax.slice_in_dim(source, lowest, lowest + (length_out - 1) * stride + 1,...  41.5 us
    dot_general x11, matrix products, along_columns(): jnp.einsum('rsc,co->rso', piece_field, table, precision=lax.Precision.HIG...  12.7 us
    dot_general x3, local copies, waits for them, and re-layouts, along_columns(): jnp.einsum('rsc,co->rso', piece_field, table, precision=lax.Precision.HIG...  11.4 us
    slice x3, local copies, waits for them, and re-layouts, smooth(): lax.slice_in_dim(source, begin_at, begin_at + (length_out - 1) * stride +...  10.5 us
    ppermute x7, starting transfers between devices, swapped_with_each(): part = lax.ppermute(part, axis, [(d, d ^ mask) for d in range(ways)])  9.67 us
    ppermute x2, starting transfers between devices, padded_2(): lax.ppermute(lax.slice_in_dim(block, block.shape[dim] - width, None, axis...  8.4 us
    add x4, other arithmetic, smooth(): result = result + weights[offset] * window  7.79 us
    ppermute x7, waiting for transfers between devices, swapped_with_each(): part = lax.ppermute(part, axis, [(d, d ^ mask) for d in range(ways)])  6 us
  transfers between devices with their start and end apart: 13, of which 1 were waited for; matrix products, arithmetic and copies ran while one was open for 19% of the time, Pallas kernels for 0%

profile of v1, /device:TPU:1, one launch (start us, length us, event | category | flops | bytes accessed | tf_op | source)
XLA Modules:
  0.0 137.4 jit_solution(4577545920242930509)
XLA Ops:
  2.8 3.0 %gather_fusion = bf16[4,128,512]{2,0,1:T(4,128)(2,1)S(1)} fusion(bf16[4,136,512]{2,0,1:T(4,128)(2,1)S(1)} %pad.20, s32[4]{0:T(128)S(1)} %fusion.514), kind=kCustom, calls=%fused_computation | custom fusion | bytes 1048624 | tf_op jit(solution)/shard_map/vmap()/gather | solution.py:81
  6.2 2.8 %collective-permute-start.1 = (bf16[1,16,4,512]{3,2,1,0:T(4,128)(2,1)S(1)}, bf16[1,16,4,512]{3,2,1,0:T(4,128)(2,1)S(1)}, u32[]{:S(2)}, u32[]{:S(2)}) collective-permute-start(bf16[1,16,4,512]{3,2,1,0:T(4,128)(2,1)S(1)} %get-tuple-element.15), channel_id=1, source_target_pairs={{0,2},{1,3},{2,0},{3,1},{4,6},{5,7},{6,4},{7,5},{8,10},{9,11},{10,... | collective-permute-start | bytes 196616 | tf_op jit(solution)/shard_map/ppermute | solution.py:23
  12.1 3.5 %collective-permute-start.5 = (bf16[1,16,4,512]{3,2,1,0:T(4,128)(2,1)S(1)}, bf16[1,16,4,512]{3,2,1,0:T(4,128)(2,1)S(1)}, u32[]{:S(2)}, u32[]{:S(2)}) collective-permute-start(bf16[1,16,4,512]{3,2,1,0:T(4,128)(2,1)S(1)} %get-tuple-element.11), channel_id=1, source_target_pairs={{0,6},{1,7},{2,4},{3,5},{4,2},{5,3},{6,0},{7,1},{8,14},{9,15},{10,... | collective-permute-start | bytes 196616 | tf_op jit(solution)/shard_map/ppermute | solution.py:23
  16.2 6.0 %collective-permute-done.4 = bf16[1,16,4,512]{3,2,1,0:T(4,128)(2,1)S(1)} collective-permute-done((bf16[1,16,4,512]{3,2,1,0:T(4,128)(2,1)S(1)}, bf16[1,16,4,512]{3,2,1,0:T(4,128)(2,1)S(1)}, u32[]{:S(2)}, u32[]{:S(2)}) %collective-permute-start.4) | collective-permute-done | bytes 65568 | tf_op jit(solution)/shard_map/ppermute | solution.py:23
  24.7 4.8 %collective-permute-start.7 = (bf16[4,32,512]{2,1,0:T(8,128)(2,1)S(1)}, bf16[4,32,512]{2,1,0:T(8,128)(2,1)S(1)}, u32[]{:S(2)}, u32[]{:S(2)}) collective-permute-start(bf16[4,32,512]{2,1,0:T(8,128)(2,1)S(1)} %get-tuple-element.8), channel_id=1, source_target_pairs={{0,1},{1,2},{2,3},{3,4},{4,5},{5,6},{6,7},{8,9},{9,10},{10,11},{11... | collective-permute-start | bytes 393224 | tf_op jit(solution)/shard_map/ppermute | solution.py:33
  33.7 3.1 %collective-permute-start.9 = (bf16[24,32,6]{2,1,0:T(8,128)(2,1)S(1)}, bf16[24,32,6]{2,1,0:T(8,128)(2,1)S(1)}, u32[]{:S(2)}, u32[]{:S(2)}) collective-permute-start(bf16[24,32,6]{2,1,0:T(8,128)(2,1)S(1)} %get-tuple-element.7), channel_id=1, source_target_pairs={{0,8},{8,16},{16,24},{1,9},{9,17},{17,25},{2,10},{10,18},{18,26},{... | collective-permute-start | bytes 27656 | tf_op jit(solution)/shard_map/ppermute | solution.py:44
  40.8 2.7 %fusion.52 = f32[24,32,512]{2,1,0:T(8,128)} fusion(bf16[4,32,512]{2,1,0:T(8,128)(2,1)S(1)} %collective-permute-done.8, bf16[16,32,512]{2,1,0:T(8,128)(2,1)S(1)} %bitcast_dynamic-update-slice_fusion, bf16[4,32,512]{2,1,0:T(8,128)(2,1)S(1)} %collective-permute-done.7), kind=kOutput, calls=%fused_computation.94 | convolution fusion | flops 2424045568 | bytes 2359296 | tf_op jit(solution)/shard_map/rsc,co->rso/dot_general | solution.py:98
  45.3 3.9 %copy.22 = f32[24,32,260]{1,0,2:T(8,128)} copy(f32[24,32,260]{2,1,0:T(8,128)S(1)} %fusion.115) | data formatting | bytes 1597440 | tf_op jit(solution)/shard_map/rsc,co->rso/dot_general | solution.py:98
  49.9 3.7 %copy.25 = f32[24,32,260]{1,0,2:T(8,128)} copy(f32[24,32,260]{2,1,0:T(8,128)S(1)} %fusion.343) | data formatting | bytes 1597440 | tf_op jit(solution)/shard_map/rsc,co->rso/dot_general | solution.py:98
  54.3 3.8 %copy.23 = f32[24,32,260]{1,0,2:T(8,128)} copy(f32[24,32,260]{2,1,0:T(8,128)S(1)} %fusion.345) | data formatting | bytes 1597440 | tf_op jit(solution)/shard_map/rsc,co->rso/dot_general | solution.py:98
  58.1 4.2 %add_add_fusion = f32[24,32,260]{1,0,2:T(8,128)S(1)} fusion(f32[24,32,260]{1,0,2:T(8,128)} %copy.25, f32[24,32,260]{1,0,2:T(8,128)} %copy.22, f32[24,32,260]{1,0,2:T(8,128)} %copy.23), kind=kLoop, calls=%fused_computation.1 | loop fusion | flops 399360 | bytes 3194880 | tf_op jit(solution)/shard_map/add | solution.py:99
  62.3 4.1 %slice.223 = f32[8,32,260]{1,0,2:T(8,128)} slice(f32[24,32,260]{1,0,2:T(8,128)S(1)} %add_add_fusion), slice={[6:21:2], [0:32:1], [0:260:1]} | slice | bytes 532480 | tf_op jit(solution)/shard_map/slice | solution.py:66
  66.4 4.0 %slice.222 = f32[8,32,260]{1,0,2:T(8,128)} slice(f32[24,32,260]{1,0,2:T(8,128)S(1)} %add_add_fusion), slice={[5:20:2], [0:32:1], [0:260:1]} | slice | bytes 532480 | tf_op jit(solution)/shard_map/slice | solution.py:66
  70.4 4.0 %slice.221 = f32[8,32,260]{1,0,2:T(8,128)} slice(f32[24,32,260]{1,0,2:T(8,128)S(1)} %add_add_fusion), slice={[4:19:2], [0:32:1], [0:260:1]} | slice | bytes 532480 | tf_op jit(solution)/shard_map/slice | solution.py:66
  74.5 4.0 %slice.220 = f32[8,32,260]{1,0,2:T(8,128)} slice(f32[24,32,260]{1,0,2:T(8,128)S(1)} %add_add_fusion), slice={[3:18:2], [0:32:1], [0:260:1]} | slice | bytes 532480 | tf_op jit(solution)/shard_map/slice | solution.py:66
  78.5 4.1 %slice.219 = f32[8,32,260]{1,0,2:T(8,128)} slice(f32[24,32,260]{1,0,2:T(8,128)S(1)} %add_add_fusion), slice={[2:17:2], [0:32:1], [0:260:1]} | slice | bytes 532480 | tf_op jit(solution)/shard_map/slice | solution.py:61
  82.6 2.8 %multiply_add_fusion.1 = f32[8,32,260]{1,0,2:T(8,128)S(1)} fusion(f32[8,32,260]{1,0,2:T(8,128)} %slice.223, f32[8,32,260]{1,0,2:T(8,128)} %slice.222, f32[8,32,260]{1,0,2:T(8,128)} %slice.221, f32[8,32,260]{1,0,2:T(8,128)} %slice.220, f32[8,32,260]{1,0,2:T(8,128)} %slice.219), kind=kLoop, calls=%fused_computation.22 | loop fusion | flops 599040 | bytes 1597440 | tf_op jit(solution)/shard_map/add | solution.py:69
  85.8 6.1 %slice.228 = f32[8,16,260]{1,0,2:T(8,128)S(1)} slice(f32[8,36,260]{1,0,2:T(8,128)S(1)} %pad.23), slice={[0:8:1], [4:35:2], [0:260:1]} | slice | bytes 266240 | tf_op jit(solution)/shard_map/slice | solution.py:66
  91.8 6.1 %slice.227 = f32[8,16,260]{1,0,2:T(8,128)S(1)} slice(f32[8,36,260]{1,0,2:T(8,128)S(1)} %pad.23), slice={[0:8:1], [3:34:2], [0:260:1]} | slice | bytes 266240 | tf_op jit(solution)/shard_map/slice | solution.py:66
  97.9 6.6 %slice.226 = f32[8,16,260]{1,0,2:T(8,128)} slice(f32[8,36,260]{1,0,2:T(8,128)S(1)} %pad.23), slice={[0:8:1], [2:33:2], [0:260:1]} | slice | bytes 266240 | tf_op jit(solution)/shard_map/slice | solution.py:66
  104.5 6.5 %slice.225 = f32[8,16,260]{1,0,2:T(8,128)} slice(f32[8,36,260]{1,0,2:T(8,128)S(1)} %pad.23), slice={[0:8:1], [1:32:2], [0:260:1]} | slice | bytes 266240 | tf_op jit(solution)/shard_map/slice | solution.py:66
  111.0 6.4 %slice.224 = f32[8,16,260]{1,0,2:T(8,128)} slice(f32[8,36,260]{1,0,2:T(8,128)S(1)} %pad.23), slice={[0:8:1], [0:31:2], [0:260:1]} | slice | bytes 266240 | tf_op jit(solution)/shard_map/slice | solution.py:61
  122.7 3.6 %collective-permute-start.11 = (f32[2,16,128]{2,1,0:T(8,128)S(1)}, f32[2,16,128]{2,1,0:T(8,128)S(1)}, u32[]{:S(2)}, u32[]{:S(2)}) collective-permute-start(f32[2,16,128]{2,1,0:T(8,128)S(1)} %get-tuple-element.17), channel_id=1, source_target_pairs={{0,1},{1,2},{2,3},{3,4},{4,5},{5,6},{6,7},{8,9},{9,10},{10,11},{11... | collective-permute-start | bytes 49160 | tf_op jit(solution)/shard_map/ppermute | solution.py:33
  133.7 3.0 %fusion.10 = bf16[16,32,512]{2,1,0:T(8,128)(2,1)} fusion(f32[16,32,512]{2,1,0:T(8,128)S(1)} %get-tuple-element.22, f32[16,32,512]{2,1,0:T(8,128)S(1)} %get-tuple-element.21), kind=kLoop, calls=%fused_computation.33 | loop fusion | flops 9437184 | bytes 2621440 | tf_op jit(solution)/shard_map/convert_element_type | solution.py:138
  (90 shorter events, 30.0 us)
Async XLA Ops:
  5.8 6.2 %copy-start.8 = (pred[4]{0:T(512)(128)(4,1)S(1)}, pred[4]{0:T(512)(128)(4,1)}, u32[]{:S(2)}) copy-start(pred[4]{0:T(512)(128)(4,1)} %constant.273) | copy-start | bytes 16
  5.8 6.2 %copy-start.9 = (pred[4]{0:T(512)(128)(4,1)S(1)}, pred[4]{0:T(512)(128)(4,1)}, u32[]{:S(2)}) copy-start(pred[4]{0:T(512)(128)(4,1)} %constant.272) | copy-start | bytes 16
  6.0 6.0 %collective-permute-start = (bf16[1,16,4,512]{3,2,1,0:T(4,128)(2,1)S(1)}, bf16[1,16,4,512]{3,2,1,0:T(4,128)(2,1)S(1)}, u32[]{:S(2)}, u32[]{:S(2)}) collective-permute-start(bf16[1,16,4,512]{3,2,1,0:T(4,128)(2,1)S(1)} %get-tuple-element.16), channel_id=1, source_target_pairs={{0,1},{1,0},{2,3},{3,2},{4,5},{5,4},{6,7},{7,6},{8,9},{9,8},{10,11... | collective-permute-start | bytes 196616 | tf_op jit(solution)/shard_map/ppermute | solution.py:23
  6.2 9.5 %collective-permute-start.1 = (bf16[1,16,4,512]{3,2,1,0:T(4,128)(2,1)S(1)}, bf16[1,16,4,512]{3,2,1,0:T(4,128)(2,1)S(1)}, u32[]{:S(2)}, u32[]{:S(2)}) collective-permute-start(bf16[1,16,4,512]{3,2,1,0:T(4,128)(2,1)S(1)} %get-tuple-element.15), channel_id=1, source_target_pairs={{0,2},{1,3},{2,0},{3,1},{4,6},{5,7},{6,4},{7,5},{8,10},{9,11},{10,... | collective-permute-start | bytes 196616 | tf_op jit(solution)/shard_map/ppermute | solution.py:23
  8.9 7.1 %collective-permute-start.2 = (bf16[1,16,4,512]{3,2,1,0:T(4,128)(2,1)S(1)}, bf16[1,16,4,512]{3,2,1,0:T(4,128)(2,1)S(1)}, u32[]{:S(2)}, u32[]{:S(2)}) collective-permute-start(bf16[1,16,4,512]{3,2,1,0:T(4,128)(2,1)S(1)} %get-tuple-element.14), channel_id=1, source_target_pairs={{0,3},{1,2},{2,1},{3,0},{4,7},{5,6},{6,5},{7,4},{8,11},{9,10},{10,... | collective-permute-start | bytes 196616 | tf_op jit(solution)/shard_map/ppermute | solution.py:23
  9.0 7.1 %collective-permute-start.3 = (bf16[1,16,4,512]{3,2,1,0:T(4,128)(2,1)S(1)}, bf16[1,16,4,512]{3,2,1,0:T(4,128)(2,1)S(1)}, u32[]{:S(2)}, u32[]{:S(2)}) collective-permute-start(bf16[1,16,4,512]{3,2,1,0:T(4,128)(2,1)S(1)} %get-tuple-element.13), channel_id=1, source_target_pairs={{0,4},{1,5},{2,6},{3,7},{4,0},{5,1},{6,2},{7,3},{8,12},{9,13},{10,... | collective-permute-start | bytes 196616 | tf_op jit(solution)/shard_map/ppermute | solution.py:23
  11.6 10.5 %collective-permute-start.4 = (bf16[1,16,4,512]{3,2,1,0:T(4,128)(2,1)S(1)}, bf16[1,16,4,512]{3,2,1,0:T(4,128)(2,1)S(1)}, u32[]{:S(2)}, u32[]{:S(2)}) collective-permute-start(bf16[1,16,4,512]{3,2,1,0:T(4,128)(2,1)S(1)} %get-tuple-element.12), channel_id=1, source_target_pairs={{0,5},{1,4},{2,7},{3,6},{4,1},{5,0},{6,3},{7,2},{8,13},{9,12},{10,... | collective-permute-start | bytes 196616 | tf_op jit(solution)/shard_map/ppermute | solution.py:23
  11.9 17.6 %copy-start.5 = (s32[3]{0:T(128)S(1)}, s32[3]{0:T(128)}, u32[]{:S(2)}) copy-start(s32[3]{0:T(128)} %param.7) | copy-start | bytes 40
  11.9 21.4 %copy-start.7 = (s32[4]{0:T(128)S(1)}, s32[4]{0:T(128)}, u32[]{:S(2)}) copy-start(s32[4]{0:T(128)} %constant.256.clone) | copy-start | bytes 52
  12.1 10.1 %collective-permute-start.5 = (bf16[1,16,4,512]{3,2,1,0:T(4,128)(2,1)S(1)}, bf16[1,16,4,512]{3,2,1,0:T(4,128)(2,1)S(1)}, u32[]{:S(2)}, u32[]{:S(2)}) collective-permute-start(bf16[1,16,4,512]{3,2,1,0:T(4,128)(2,1)S(1)} %get-tuple-element.11), channel_id=1, source_target_pairs={{0,6},{1,7},{2,4},{3,5},{4,2},{5,3},{6,0},{7,1},{8,14},{9,15},{10,... | collective-permute-start | bytes 196616 | tf_op jit(solution)/shard_map/ppermute | solution.py:23
  15.7 6.6 %collective-permute-start.6 = (bf16[1,16,4,512]{3,2,1,0:T(4,128)(2,1)S(1)}, bf16[1,16,4,512]{3,2,1,0:T(4,128)(2,1)S(1)}, u32[]{:S(2)}, u32[]{:S(2)}) collective-permute-start(bf16[1,16,4,512]{3,2,1,0:T(4,128)(2,1)S(1)} %get-tuple-element.10), channel_id=1, source_target_pairs={{0,7},{1,6},{2,5},{3,4},{4,3},{5,2},{6,1},{7,0},{8,15},{9,14},{10,... | collective-permute-start | bytes 196616 | tf_op jit(solution)/shard_map/ppermute | solution.py:23
  22.4 11.0 %collective-permute-start.8 = (bf16[4,32,512]{2,1,0:T(8,128)(2,1)S(1)}, bf16[4,32,512]{2,1,0:T(8,128)(2,1)S(1)}, u32[]{:S(2)}, u32[]{:S(2)}) collective-permute-start(bf16[4,32,512]{2,1,0:T(8,128)(2,1)S(1)} %get-tuple-element.9), channel_id=1, source_target_pairs={{1,0},{2,1},{3,2},{4,3},{5,4},{6,5},{7,6},{9,8},{10,9},{11,10},{12... | collective-permute-start | bytes 393224 | tf_op jit(solution)/shard_map/ppermute | solution.py:36
  24.7 8.7 %collective-permute-start.7 = (bf16[4,32,512]{2,1,0:T(8,128)(2,1)S(1)}, bf16[4,32,512]{2,1,0:T(8,128)(2,1)S(1)}, u32[]{:S(2)}, u32[]{:S(2)}) collective-permute-start(bf16[4,32,512]{2,1,0:T(8,128)(2,1)S(1)} %get-tuple-element.8), channel_id=1, source_target_pairs={{0,1},{1,2},{2,3},{3,4},{4,5},{5,6},{6,7},{8,9},{9,10},{10,11},{11... | collective-permute-start | bytes 393224 | tf_op jit(solution)/shard_map/ppermute | solution.py:33
  33.7 19.9 %collective-permute-start.9 = (bf16[24,32,6]{2,1,0:T(8,128)(2,1)S(1)}, bf16[24,32,6]{2,1,0:T(8,128)(2,1)S(1)}, u32[]{:S(2)}, u32[]{:S(2)}) collective-permute-start(bf16[24,32,6]{2,1,0:T(8,128)(2,1)S(1)} %get-tuple-element.7), channel_id=1, source_target_pairs={{0,8},{8,16},{16,24},{1,9},{9,17},{17,25},{2,10},{10,18},{18,26},{... | collective-permute-start | bytes 27656 | tf_op jit(solution)/shard_map/ppermute | solution.py:44
  36.8 12.4 %collective-permute-start.10 = (bf16[24,32,6]{2,1,0:T(8,128)(2,1)S(1)}, bf16[24,32,6]{2,1,0:T(8,128)(2,1)S(1)}, u32[]{:S(2)}, u32[]{:S(2)}) collective-permute-start(bf16[24,32,6]{2,1,0:T(8,128)(2,1)S(1)} %get-tuple-element.6), channel_id=1, source_target_pairs={{8,0},{16,8},{24,16},{9,1},{17,9},{25,17},{10,2},{18,10},{26,18},{... | collective-permute-start | bytes 27656 | tf_op jit(solution)/shard_map/ppermute | solution.py:44
  53.6 0.7 copy-start
  119.6 0.8 copy-start.6
  119.7 6.7 %copy-start.1 = (bf16[24,32,6]{2,1,0:T(8,128)(2,1)S(1)}, bf16[24,32,6]{2,1,0:T(8,128)(2,1)}, u32[]{:S(2)}) copy-start(bf16[24,32,6]{2,1,0:T(8,128)(2,1)} %copy-done) | copy-start | bytes 27652
  120.0 7.1 %copy-start.4 = (bf16[8,16,256]{2,1,0:T(8,128)(2,1)}, bf16[8,16,256]{2,1,0:T(8,128)(2,1)S(1)}, u32[]{:S(2)}) copy-start(bf16[8,16,256]{2,1,0:T(8,128)(2,1)S(1)} %copy.28) | copy-start | bytes 196612
  120.7 16.0 %collective-permute-start.12 = (f32[2,16,128]{2,1,0:T(8,128)S(1)}, f32[2,16,128]{2,1,0:T(8,128)S(1)}, u32[]{:S(2)}, u32[]{:S(2)}) collective-permute-start(f32[2,16,128]{2,1,0:T(8,128)S(1)} %get-tuple-element.18), channel_id=1, source_target_pairs={{1,0},{2,1},{3,2},{4,3},{5,4},{6,5},{7,6},{9,8},{10,9},{11,10},{12... | collective-permute-start | bytes 49160 | tf_op jit(solution)/shard_map/ppermute | solution.py:36
  122.7 14.0 %collective-permute-start.11 = (f32[2,16,128]{2,1,0:T(8,128)S(1)}, f32[2,16,128]{2,1,0:T(8,128)S(1)}, u32[]{:S(2)}, u32[]{:S(2)}) collective-permute-start(f32[2,16,128]{2,1,0:T(8,128)S(1)} %get-tuple-element.17), channel_id=1, source_target_pairs={{0,1},{1,2},{2,3},{3,4},{4,5},{5,6},{6,7},{8,9},{9,10},{10,11},{11... | collective-permute-start | bytes 49160 | tf_op jit(solution)/shard_map/ppermute | solution.py:33
  127.2 1.4 %copy-start.3 = (f32[24,32,512]{2,1,0:T(8,128)S(1)}, f32[24,32,512]{2,1,0:T(8,128)}, u32[]{:S(2)}) copy-start(f32[24,32,512]{2,1,0:T(8,128)} %fusion.50) | copy-start | bytes 4718596
  128.6 1.4 %copy-start.2 = (f32[24,32,512]{2,1,0:T(8,128)S(1)}, f32[24,32,512]{2,1,0:T(8,128)}, u32[]{:S(2)}) copy-start(f32[24,32,512]{2,1,0:T(8,128)} %fusion.52) | copy-start | bytes 4718596
